TPU v7x, 256 devices: a whole 4x4x8 slice. The times are simulated.
256 devices in a mesh: seq: 64 (over z, x, core), tp: 4 (over y).
Axes of the slice: x: 4, y: 4, z: 8, core: 2. Of those that a mesh axis runs over, the one named last changes fastest.
Arguments:
- layer_input: bfloat16 [16384, 2048], P('seq'), may hold values from -1.5 to 1.5
- norm_gain: float32 [2048], replicated, may hold values from 0.5 to 1.5
- w_query: bfloat16 [2048, 2048], P(None, 'tp')
- key_weight: bfloat16 [2048, 1024], P(None, 'tp')
- value_weight: bfloat16 [2048, 1024], P(None, 'tp'), may hold values from -0.125 to 0.125
- w_out: bfloat16 [2048, 2048], P('tp'), may hold values from -1 to 1
- query_gain: float32 [128], replicated, may hold values from 0.6 to 6, as said below
- key_gain: float32 [128], replicated, may hold values from 0.6 to 6, as said below
- seg_ids: int32 [16384], P('seq'), may hold values from 0 to 7, as said below
- positions: int32 [16384], P('seq'), may hold values from 0 to 13106, as said below
- post_gain: float32 [2048], replicated, may hold values from 0.5 to 1.5
- w_gate: bfloat16 [2048, 3072], P('seq', 'tp'), may hold values from -0.125 to 0.125
- w_up: bfloat16 [2048, 3072], P('seq', 'tp'), may hold values from -0.125 to 0.125
- w_down: bfloat16 [3072, 2048], P('tp', 'seq'), may hold values from -0.21875 to 0.21875
Outputs:
- hidden: bfloat16 [16384, 2048], P('seq')
- key_cache: bfloat16 [16384, 1024], P('seq', 'tp')
- value_cache: bfloat16 [16384, 1024], P('seq', 'tp')
Inputs may be any that keep to these rules, and one draw needn't show every extreme that they name: `seg_ids`: prompt numbers never fall along the stream; each of the 8 prompts is a contiguous run of one or more tokens, and one prompt has exactly 13107 tokens. `positions`: each token's place in its prompt, counting from 0 at the prompt's first token. `query_gain`: positive gains. `key_gain`: positive gains.
All inputs are finite; a program needn't handle non-finite values.
Results may differ from a plain program's by a relative error of at most 0.02.
Values may be sent and summed in bfloat16 or wider, within the bound.
A program may use at most 128 MiB of HBM per device.

v0:
```python
import math
import jax
import jax.numpy as jnp
from jax import lax
from jax.sharding import PartitionSpec as P


def rms(v, gain):
    return v * lax.rsqrt(jnp.mean(v * v, axis=-1, keepdims=True) + 1e-06) * gain


def rope(v, place):
    half = v.shape[-1] // 2
    freqs = 1000000.0 ** (-2.0 * jnp.arange(half, dtype=jnp.float32) / v.shape[-1])
    angle = place.astype(jnp.float32)[:, None] * freqs[None, :]
    cosine = jnp.cos(angle)[:, None, :]
    sine = jnp.sin(angle)[:, None, :]
    block_start = v[..., :half]
    second = v[..., half:]
    return jnp.concatenate(
        [block_start * cosine - second * sine, second * cosine + block_start * sine], axis=-1
    )


def body(
    layer_input,
    norm_gain,
    w_query,
    key_weight,
    value_weight,
    w_out,
    query_gain,
    key_gain,
    seg_ids,
    positions,
    post_gain,
    w_gate,
    w_up,
    w_down,
):
    rows = layer_input.shape[0]
    head_size = query_gain.shape[0]
    query_local = w_query.shape[1] // head_size
    kv_local = key_weight.shape[1] // head_size
    head_group = query_local // kv_local
    scale = 1.0 / math.sqrt(head_size)
    xf = layer_input.astype(jnp.float32)
    normed_input = rms(xf, norm_gain).astype(jnp.bfloat16)
    query_matrix = jnp.dot(normed_input, w_query, preferred_element_type=jnp.float32).reshape(
        rows, query_local, head_size
    )
    query_matrix = rope(rms(query_matrix, query_gain), positions).astype(jnp.bfloat16)
    key_matrix = jnp.dot(normed_input, key_weight, preferred_element_type=jnp.float32).reshape(
        rows, kv_local, head_size
    )
    key_matrix = rope(rms(key_matrix, key_gain), positions).astype(jnp.bfloat16)
    key_cache = key_matrix.reshape(rows, kv_local * head_size)
    value_cache = jnp.dot(normed_input, value_weight, preferred_element_type=jnp.float32).astype(
        jnp.bfloat16
    )
    grouped = query_matrix.reshape(rows, kv_local, head_group, head_size).transpose(1, 2, 0, 3)
    me = lax.axis_index("seq")
    my_last = me * rows + rows - 1

    def update(state, key_rows, value_rows, seg_rows, place_rows):
        top, total, acc = state
        count = key_rows.shape[0]
        s = (
            jnp.einsum(
                "hgqd,khd->hgqk",
                grouped,
                key_rows.reshape(count, kv_local, head_size),
                preferred_element_type=jnp.float32,
            )
            * scale
        )
        allowed = (seg_ids[:, None] == seg_rows[None, :]) & (
            place_rows[None, :] <= positions[:, None]
        )
        s = jnp.where(allowed, s, -1e30)
        new_top = jnp.maximum(top, jnp.max(s, axis=-1))
        p = jnp.where(allowed, jnp.exp(s - new_top[..., None]), 0.0)
        decay = jnp.exp(top - new_top)
        total = total * decay + jnp.sum(p, axis=-1)
        acc = acc * decay[..., None] + jnp.einsum(
            "hgqk,khd->hgqd",
            p.astype(jnp.bfloat16),
            value_rows.reshape(count, kv_local, head_size),
            preferred_element_type=jnp.float32,
        )
        return (new_top, total, acc)

    start_state = (
        jnp.full((kv_local, head_group, rows), -1e30, jnp.float32),
        jnp.zeros((kv_local, head_group, rows), jnp.float32),
        jnp.zeros((kv_local, head_group, rows, head_size), jnp.float32),
    )
    travel = (key_cache, value_cache, seg_ids, positions)
    dead = jnp.int32(0) < 0
    key_rows = lax.all_gather(travel[0], "seq", axis=0, tiled=True)
    value_rows = lax.all_gather(travel[1], "seq", axis=0, tiled=True)
    seg_rows = lax.all_gather(travel[2], "seq", axis=0, tiled=True)
    place_rows = lax.all_gather(travel[3], "seq", axis=0, tiled=True)
    count = key_rows.shape[0]
    shards = count // rows
    limit = max(1, 1024 // rows)
    factor = 1
    for trial in range(1, limit + 1):
        if shards % trial == 0:
            factor = trial
    width = rows * factor

    def one_block(step, inner):
        offset = step * width
        kb = lax.dynamic_slice_in_dim(key_rows, offset, width, 0)
        vb = lax.dynamic_slice_in_dim(value_rows, offset, width, 0)
        sb = lax.dynamic_slice_in_dim(seg_rows, offset, width, 0)
        pb = lax.dynamic_slice_in_dim(place_rows, offset, width, 0)
        skip = dead | (offset > my_last) | (sb[width - 1] < seg_ids[0])
        return lax.cond(skip, lambda c: c, lambda c: update(c, kb, vb, sb, pb), inner)

    top, total, acc = lax.fori_loop(0, count // width, one_block, start_state)
    attended = (acc / total[..., None]).astype(jnp.bfloat16)
    attended = attended.transpose(2, 0, 1, 3).reshape(rows, query_local * head_size)
    partial_out = jnp.dot(attended, w_out, preferred_element_type=jnp.float32)
    summed = lax.psum(partial_out.astype(jnp.bfloat16), "tp").astype(jnp.float32)
    mid = (xf + summed).astype(jnp.bfloat16)
    mid_f = mid.astype(jnp.float32)
    post_normed = rms(mid_f, post_gain).astype(jnp.bfloat16)
    gate = jnp.dot(
        post_normed,
        lax.all_gather(w_gate, "seq", axis=0, tiled=True),
        preferred_element_type=jnp.float32,
    )
    up = jnp.dot(
        post_normed,
        lax.all_gather(w_up, "seq", axis=0, tiled=True),
        preferred_element_type=jnp.float32,
    )
    act = (jax.nn.silu(gate) * up).astype(jnp.bfloat16)
    terms = jnp.dot(
        act, lax.all_gather(w_down, "seq", axis=1, tiled=True), preferred_element_type=jnp.float32
    )
    ffn_total = lax.psum(terms.astype(jnp.bfloat16), "tp").astype(jnp.float32)
    hidden = (mid_f + ffn_total).astype(jnp.bfloat16)
    return (hidden, key_cache, value_cache)


def solution(mesh):
    in_specs = (
        P("seq", None),
        P(),
        P(None, "tp"),
        P(None, "tp"),
        P(None, "tp"),
        P("tp", None),
        P(),
        P(),
        P("seq"),
        P("seq"),
        P(),
        P("seq", "tp"),
        P("seq", "tp"),
        P("tp", "seq"),
    )
    out_specs = (P("seq", None), P("seq", "tp"), P("seq", "tp"))
    return jax.shard_map(body, mesh=mesh, in_specs=in_specs, out_specs=out_specs, check_vma=False)
```

profile of v0, /device:TPU:2, one launch (start us, length us, event | category | flops | bytes accessed | tf_op | source)
XLA Modules:
  0.0 657.9 jit_solution(4688254087747547651)
XLA Ops:
  7.3 1.6 fusion.12
  8.9 3.0 multiply_reduce_fusion.1
  12.0 0.5 multiply_cosine_fusion
  12.7 1.0 multiply_multiply_fusion.1
  13.8 0.8 copy.77
  14.6 2.4 convolution_convert_fusion.2
  17.1 3.2 fusion.28
  20.3 1.2 reshape.128
  22.2 0.5 subtract_convert_fusion
  22.8 46.4 %all-gather = s32[64,1,256]{2,1,0:T(1,128)S(1)} all-gather(s32[1,1,256]{2,1,0:T(1,128)S(1)} %bitcast.61), channel_id=1, replica_groups=mesh['seq'=64,'tp'=4] {'seq'}, dimensions={0}, use_global_device_ids=true | all-gather | bytes 66560 | tf_op jit(solution)/shard_map/all_gather | solution.py:102
  69.2 41.5 %all-gather.1 = s32[64,1,256]{2,1,0:T(1,128)S(1)} all-gather(s32[1,1,256]{2,1,0:T(1,128)S(1)} %bitcast.60), channel_id=1, replica_groups=mesh['seq'=64,'tp'=4] {'seq'}, dimensions={0}, use_global_device_ids=true | all-gather | bytes 66560 | tf_op jit(solution)/shard_map/all_gather | solution.py:103
  110.9 11.9 %copy.67 = bf16[16384,256]{0,1:T(8,128)(2,1)} copy(bf16[16384,256]{1,0:T(8,128)(2,1)} %all-gather.8.cloned.1.call-done) | data formatting | bytes 16777216 | tf_op jit(solution)/shard_map/while | solution.py:122
  122.8 60.4 %all-gather.10.cloned.1.call-done = bf16[16384,256]{1,0:T(8,128)(2,1)} async-done(((bf16[256,256]{1,0:T(8,128)(2,1)}), bf16[16384,256]{1,0:T(8,128)(2,1)}) %all-gather.10.cloned.1.call-update) | async-done | bytes 8388624 | tf_op jit(solution)/shard_map/all_gather | solution.py:101
  183.2 11.8 %copy.68 = bf16[16384,256]{0,1:T(8,128)(2,1)} copy(bf16[16384,256]{1,0:T(8,128)(2,1)} %all-gather.10.cloned.1.call-done) | data formatting | bytes 16777216 | tf_op jit(solution)/shard_map/while | solution.py:122
  195.0 44.5 %while.17 = (s32[]{:T(128)}, f32[2,2,256]{2,1,0:T(2,128)S(1)}, f32[2,2,256]{2,1,0:T(2,128)S(1)}, f32[2,2,256,128]{3,2,1,0:T(8,128)S(1)}, s32[]{:T(128)}, /*index...) while((s32[]{:T(128)}, f32[2,2,256]{2,1,0:T(2,128)S(1)}, ...), condition=%wide.region_8.9_spmd, body=%wide.region_3.8_spmd.sunk | while | flops 551553024 | bytes 18180480 | solution.py:122
  195.1 0.6 slice.44
  195.7 0.5 slice.45
  197.4 5.3 conditional.2
  197.8 1.3 constant_dynamic-slice_fusion
  199.1 0.9 fusion
  200.0 1.0 fusion.2
  201.1 1.6 fusion.6
  202.8 0.6 slice.44
  203.4 0.5 slice.45
  205.2 0.6 slice.44
  205.9 0.5 slice.45
  207.7 0.6 slice.44
  208.3 0.5 slice.45
  210.1 0.6 slice.44
  210.8 0.5 slice.45
  212.6 0.6 slice.44
  213.2 0.5 slice.45
  215.1 0.6 slice.44
  215.7 0.5 slice.45
  217.5 0.6 slice.44
  218.2 0.5 slice.45
  220.0 0.6 slice.44
  220.6 0.5 slice.45
  222.4 0.6 slice.44
  223.1 0.5 slice.45
  224.9 0.6 slice.44
  225.5 0.5 slice.45
  227.3 0.6 slice.44
  228.0 0.5 slice.45
  229.8 0.6 slice.44
  230.4 0.5 slice.45
  232.2 0.6 slice.44
  234.7 0.6 slice.44
  235.3 0.5 slice.45
  237.1 0.6 slice.44
  237.8 0.5 slice.45
  239.8 1.7 convolution_convert_fusion
  241.6 0.5 all-gather.12.cloned.1.call-update
  242.2 0.5 all-gather.14.cloned.1.call-update
  242.8 0.5 all-gather.16.cloned.1.call-update
  243.5 110.3 %all-reduce.3.cloned.1.call-done = bf16[256,2048]{1,0:T(8,128)(2,1)} async-done(((bf16[256,2048]{1,0:T(8,128)(2,1)}), bf16[256,2048]{1,0:T(8,128)(2,1)}) %all-reduce.3.cloned.1.call-update) | async-done | bytes 1048592 | tf_op jit(solution)/shard_map/psum | solution.py:126
  353.8 2.0 fusion.16
  355.9 78.9 %all-gather.12.cloned.1.call-done = bf16[2048,768]{1,0:T(8,128)(2,1)} async-done(((bf16[32,768]{1,0:T(8,128)(2,1)}), bf16[2048,768]{1,0:T(8,128)(2,1)}) %all-gather.12.cloned.1.call-update) | async-done | bytes 3145744 | tf_op jit(solution)/shard_map/all_gather | solution.py:132
  434.8 3.8 fusion.24
  438.6 75.0 %all-gather.14.cloned.1.call-done = bf16[2048,768]{1,0:T(8,128)(2,1)} async-done(((bf16[32,768]{1,0:T(8,128)(2,1)}), bf16[2048,768]{1,0:T(8,128)(2,1)}) %all-gather.14.cloned.1.call-update) | async-done | bytes 3145744 | tf_op jit(solution)/shard_map/all_gather | solution.py:137
  513.6 78.8 %all-gather.16.cloned.1.call-done = bf16[768,2048]{0,1:T(8,128)(2,1)} async-done(((bf16[768,32]{0,1:T(8,128)(2,1)}), bf16[768,2048]{0,1:T(8,128)(2,1)}) %all-gather.16.cloned.1.call-update) | async-done | bytes 3145744 | tf_op jit(solution)/shard_map/all_gather | solution.py:142
  592.4 6.2 convolution_convert_fusion.1
  598.7 49.8 %all-reduce.5.cloned.1.call-done = bf16[256,2048]{1,0:T(8,128)(2,1)} async-done(((bf16[256,2048]{1,0:T(8,128)(2,1)}), bf16[256,2048]{1,0:T(8,128)(2,1)}) %all-reduce.5.cloned.1.call-update) | async-done | bytes 1048592 | tf_op jit(solution)/shard_map/psum | solution.py:144
  648.5 2.6 fusion.19
  (113 shorter events, 3.6 us)
Async XLA Ops:
  7.2 232.6 %copy-start = (bf16[512,2048]{1,0:T(8,128)(2,1)S(1)}, bf16[512,2048]{1,0:T(8,128)(2,1)}, u32[]{:S(2)}) copy-start(bf16[512,2048]{1,0:T(8,128)(2,1)} %param.23) | copy-start | bytes 6291460
  7.2 4.8 copy-start.2
  7.2 103.7 %all-gather.8.cloned.1.call-start = ((), (), s32[]{:S(2)}) async-start(), calls=%async_computation | async-start | bytes 8519680 | tf_op jit(solution)/shard_map/all_gather | solution.py:100
  8.9 3.8 copy-start.4
  8.9 5.7 copy-start.1
  14.6 168.6 %all-gather.10.cloned.1.call-start = ((), (), s32[]{:S(2)}) async-start(), calls=%async_computation.1 | async-start | bytes 8519680 | tf_op jit(solution)/shard_map/all_gather | solution.py:101
  17.0 336.8 %all-reduce.3.cloned.1.call-start = ((), (), s32[]{:S(2)}) async-start(), calls=%async_computation.2 | async-start | bytes 2097152 | tf_op jit(solution)/shard_map/psum | solution.py:126
  17.1 4.8 copy-start.5
  21.9 1.0 copy-start.3
  241.5 193.3 %copy-start.6 = (f32[2048]{0:T(1024)S(1)}, f32[2048]{0:T(1024)}, u32[]{:S(2)}) copy-start(f32[2048]{0:T(1024)} %param.28) | copy-start | bytes 24580
  241.5 193.3 %all-gather.12.cloned.1.call-start = ((), (), s32[]{:S(2)}) async-start(), calls=%async_computation.3 | async-start | bytes 3194880 | tf_op jit(solution)/shard_map/all_gather | solution.py:132
  242.1 271.5 %all-gather.14.cloned.1.call-start = ((), (), s32[]{:S(2)}) async-start(), calls=%async_computation.4 | async-start | bytes 3194880 | tf_op jit(solution)/shard_map/all_gather | solution.py:137
  242.7 349.7 %all-gather.16.cloned.1.call-start = ((), (), s32[]{:S(2)}) async-start(), calls=%async_computation.5 | async-start | bytes 3194880 | tf_op jit(solution)/shard_map/all_gather | solution.py:142
  243.3 405.2 %all-reduce.5.cloned.1.call-start = ((), (), s32[]{:S(2)}) async-start(), calls=%async_computation.6 | async-start | bytes 2097152 | tf_op jit(solution)/shard_map/psum | solution.py:144
Sparse Core Ops, SparseCore 0:
  14.7 84.7 all-gather.7
  102.8 80.3 all-gather.9
  241.7 112.1 all-reduce.2
  356.8 77.9 all-gather.11
  437.8 75.7 all-gather.13
  516.6 75.7 all-gather.15
  598.8 49.6 all-reduce.4
where the time goes:
time: 659 us; the launch traced here: 658 us
  waiting for transfers between devices  455 us (69%)
  blocking collectives  87.9 us (13%)
  local copies, waits for them, and re-layouts  45.7 us (7%)
  matrix products  22.9 us (3%)
  loops' own time  21 us (3%)
  between operations  14.4 us (2%)
  other arithmetic  10.7 us (2%)
    psum x1, waiting for transfers between devices, body(): lax.psum(partial_out.astype(jnp.bfloat16), 'tp').astype(jnp.float32)  110 us
    all_gather x1, waiting for transfers between devices, body(): lax.all_gather(w_gate, 'seq', axis=0, tiled=True)  78.9 us
    all_gather x1, waiting for transfers between devices, body(): lax.all_gather(w_down, 'seq', axis=1, tiled=True)  78.8 us
    all_gather x1, waiting for transfers between devices, body(): lax.all_gather(w_up, 'seq', axis=0, tiled=True)  75 us
    all_gather x1, waiting for transfers between devices, body(): value_rows = lax.all_gather(travel[1], 'seq', axis=0, tiled=True)  60.4 us
    psum x1, waiting for transfers between devices, body(): ffn_total = lax.psum(terms.astype(jnp.bfloat16), 'tp').astype(jnp.float32)  49.8 us
    all_gather x1, blocking collectives, body(): seg_rows = lax.all_gather(travel[2], 'seq', axis=0, tiled=True)  46.4 us
    all_gather x1, blocking collectives, body(): place_rows = lax.all_gather(travel[3], 'seq', axis=0, tiled=True)  41.5 us
  transfers between devices with their start and end apart: 7, of which 6 were waited for; matrix products, arithmetic and copies ran while one was open for 4% of the time, Pallas kernels for 0%

commit v1 on v0

--- a/solution.py
+++ b/solution.py
@@ -123,7 +123,9 @@
     attended = (acc / total[..., None]).astype(jnp.bfloat16)
     attended = attended.transpose(2, 0, 1, 3).reshape(rows, query_local * head_size)
     partial_out = jnp.dot(attended, w_out, preferred_element_type=jnp.float32)
-    summed = lax.psum(partial_out.astype(jnp.bfloat16), "tp").astype(jnp.float32)
+    summed = jnp.sum(lax.all_gather(partial_out.astype(jnp.bfloat16), "tp"), axis=0).astype(
+        jnp.float32
+    )
     mid = (xf + summed).astype(jnp.bfloat16)
     mid_f = mid.astype(jnp.float32)
     post_normed = rms(mid_f, post_gain).astype(jnp.bfloat16)

time: 659 us -> 658 us (level)
    psum x1 -> x0, waiting for transfers between devices: 110 us -> none  [body(): lax.psum(partial_out.astype(jnp.bfloat16), 'tp').astype(jnp.float32)]
    all_gather x0 -> x1, waiting for transfers between devices: none -> 110 us  [body(): lax.all_gather(partial_out.astype(jnp.bfloat16), 'tp')]
  transfers between devices with their start and end apart: 7 -> 7, of which waited for: 6 -> 6; matrix products, arithmetic and copies ran while one was open for 4% -> 5% of each run, Pallas kernels for 0% -> 0%
where the time goes in v1:
time: 658 us; the launch traced here: 656 us
  waiting for transfers between devices  449 us (68%)
  blocking collectives  87.9 us (13%)
  local copies, waits for them, and re-layouts  45.7 us (7%)
  matrix products  22.8 us (3%)
  loops' own time  21 us (3%)
  other arithmetic  15 us (2%)
  between operations  14.4 us (2%)
    all_gather x1, waiting for transfers between devices, body(): lax.all_gather(partial_out.astype(jnp.bfloat16), 'tp')  110 us
    all_gather x1, waiting for transfers between devices, body(): lax.all_gather(w_down, 'seq', axis=1, tiled=True)  78.4 us
    all_gather x1, waiting for transfers between devices, body(): lax.all_gather(w_up, 'seq', axis=0, tiled=True)  74.6 us
    all_gather x1, waiting for transfers between devices, body(): lax.all_gather(w_gate, 'seq', axis=0, tiled=True)  73.8 us
    all_gather x1, waiting for transfers between devices, body(): value_rows = lax.all_gather(travel[1], 'seq', axis=0, tiled=True)  60.4 us
    psum x1, waiting for transfers between devices, body(): ffn_total = lax.psum(terms.astype(jnp.bfloat16), 'tp').astype(jnp.float32)  49.8 us
    all_gather x1, blocking collectives, body(): seg_rows = lax.all_gather(travel[2], 'seq', axis=0, tiled=True)  46.4 us
    all_gather x1, blocking collectives, body(): place_rows = lax.all_gather(travel[3], 'seq', axis=0, tiled=True)  41.5 us
  transfers between devices with their start and end apart: 7, of which 6 were waited for; matrix products, arithmetic and copies ran while one was open for 5% of the time, Pallas kernels for 0%

profile of v1, /device:TPU:2, one launch (start us, length us, event | category | flops | bytes accessed | tf_op | source)
XLA Modules:
  0.0 656.1 jit_solution(5143650675948523525)
XLA Ops:
  7.3 1.7 fusion.12
  8.9 2.9 multiply_reduce_fusion.1
  11.9 0.5 multiply_cosine_fusion
  12.6 1.0 multiply_multiply_fusion.1
  13.7 0.8 copy.77
  14.6 2.4 convolution_convert_fusion.2
  17.0 3.2 fusion.28
  20.2 1.2 reshape.128
  22.2 0.5 subtract_convert_fusion
  22.8 46.4 %all-gather.1 = s32[64,1,256]{2,1,0:T(1,128)S(1)} all-gather(s32[1,1,256]{2,1,0:T(1,128)S(1)} %bitcast.63), channel_id=1, replica_groups=mesh['seq'=64,'tp'=4] {'seq'}, dimensions={0}, use_global_device_ids=true | all-gather | bytes 66560 | tf_op jit(solution)/shard_map/all_gather | solution.py:102
  69.2 41.5 %all-gather.2 = s32[64,1,256]{2,1,0:T(1,128)S(1)} all-gather(s32[1,1,256]{2,1,0:T(1,128)S(1)} %bitcast.62), channel_id=1, replica_groups=mesh['seq'=64,'tp'=4] {'seq'}, dimensions={0}, use_global_device_ids=true | all-gather | bytes 66560 | tf_op jit(solution)/shard_map/all_gather | solution.py:103
  110.8 11.9 %copy.67 = bf16[16384,256]{0,1:T(8,128)(2,1)} copy(bf16[16384,256]{1,0:T(8,128)(2,1)} %all-gather.10.cloned.1.call-done) | data formatting | bytes 16777216 | tf_op jit(solution)/shard_map/while | solution.py:122
  122.7 60.4 %all-gather.12.cloned.1.call-done = bf16[16384,256]{1,0:T(8,128)(2,1)} async-done(((bf16[256,256]{1,0:T(8,128)(2,1)}), bf16[16384,256]{1,0:T(8,128)(2,1)}) %all-gather.12.cloned.1.call-update) | async-done | bytes 8388624 | tf_op jit(solution)/shard_map/all_gather | solution.py:101
  183.1 11.8 %copy.68 = bf16[16384,256]{0,1:T(8,128)(2,1)} copy(bf16[16384,256]{1,0:T(8,128)(2,1)} %all-gather.12.cloned.1.call-done) | data formatting | bytes 16777216 | tf_op jit(solution)/shard_map/while | solution.py:122
  194.9 44.5 %while.17 = (s32[]{:T(128)}, f32[2,2,256]{2,1,0:T(2,128)S(1)}, f32[2,2,256]{2,1,0:T(2,128)S(1)}, f32[2,2,256,128]{3,2,1,0:T(8,128)S(1)}, s32[]{:T(128)}, /*index...) while((s32[]{:T(128)}, f32[2,2,256]{2,1,0:T(2,128)S(1)}, ...), condition=%wide.region_8.9_spmd, body=%wide.region_3.8_spmd.sunk | while | flops 551553024 | bytes 18180480 | solution.py:122
  195.0 0.6 slice.44
  195.6 0.5 slice.45
  197.3 5.3 conditional.2
  197.7 1.3 constant_dynamic-slice_fusion
  199.0 0.9 fusion
  200.0 1.0 fusion.2
  201.0 1.6 fusion.6
  202.7 0.6 slice.44
  203.4 0.5 slice.45
  205.2 0.6 slice.44
  205.8 0.5 slice.45
  207.6 0.6 slice.44
  208.3 0.5 slice.45
  210.1 0.6 slice.44
  210.7 0.5 slice.45
  212.5 0.6 slice.44
  213.2 0.5 slice.45
  215.0 0.6 slice.44
  215.6 0.5 slice.45
  217.4 0.6 slice.44
  218.1 0.5 slice.45
  219.9 0.6 slice.44
  220.5 0.5 slice.45
  222.3 0.6 slice.44
  223.0 0.5 slice.45
  224.8 0.6 slice.44
  225.4 0.5 slice.45
  227.2 0.6 slice.44
  227.9 0.5 slice.45
  229.7 0.6 slice.44
  232.1 0.6 slice.44
  234.6 0.6 slice.44
  235.2 0.5 slice.45
  237.1 0.6 slice.44
  237.7 0.5 slice.45
  239.7 1.7 convolution_convert_fusion
  241.5 0.5 all-gather.14.cloned.1.call-update
  242.1 0.5 all-gather.16.cloned.1.call-update
  242.7 0.5 all-gather.18.cloned.1.call-update
  243.4 110.2 %all-gather.20.cloned.1.call-done = bf16[1024,2048]{1,0:T(8,128)(2,1)} async-done(((bf16[256,2048]{1,0:T(8,128)(2,1)}), bf16[1024,2048]{1,0:T(8,128)(2,1)}) %all-gather.20.cloned.1.call-update) | async-done | bytes 4194320 | tf_op jit(solution)/shard_map/all_gather | solution.py:126
  353.7 4.2 reduce_sum.62
  357.9 2.0 fusion.16
  360.0 73.8 %all-gather.14.cloned.1.call-done = bf16[2048,768]{1,0:T(8,128)(2,1)} async-done(((bf16[32,768]{1,0:T(8,128)(2,1)}), bf16[2048,768]{1,0:T(8,128)(2,1)}) %all-gather.14.cloned.1.call-update) | async-done | bytes 3145744 | tf_op jit(solution)/shard_map/all_gather | solution.py:134
  433.8 3.8 fusion.24
  437.6 74.6 %all-gather.16.cloned.1.call-done = bf16[2048,768]{1,0:T(8,128)(2,1)} async-done(((bf16[32,768]{1,0:T(8,128)(2,1)}), bf16[2048,768]{1,0:T(8,128)(2,1)}) %all-gather.16.cloned.1.call-update) | async-done | bytes 3145744 | tf_op jit(solution)/shard_map/all_gather | solution.py:139
  512.2 78.4 %all-gather.18.cloned.1.call-done = bf16[768,2048]{0,1:T(8,128)(2,1)} async-done(((bf16[768,32]{0,1:T(8,128)(2,1)}), bf16[768,2048]{0,1:T(8,128)(2,1)}) %all-gather.18.cloned.1.call-update) | async-done | bytes 3145744 | tf_op jit(solution)/shard_map/all_gather | solution.py:144
  590.6 6.2 convolution_convert_fusion.1
  596.9 49.8 %all-reduce.2.cloned.1.call-done = bf16[256,2048]{1,0:T(8,128)(2,1)} async-done(((bf16[256,2048]{1,0:T(8,128)(2,1)}), bf16[256,2048]{1,0:T(8,128)(2,1)}) %all-reduce.2.cloned.1.call-update) | async-done | bytes 1048592 | tf_op jit(solution)/shard_map/psum | solution.py:146
  646.6 2.6 fusion.19
  (114 shorter events, 4.0 us)
Async XLA Ops:
  7.2 232.6 %copy-start = (bf16[512,2048]{1,0:T(8,128)(2,1)S(1)}, bf16[512,2048]{1,0:T(8,128)(2,1)}, u32[]{:S(2)}) copy-start(bf16[512,2048]{1,0:T(8,128)(2,1)} %param.23) | copy-start | bytes 6291460
  7.2 4.7 copy-start.2
  7.2 5.4 copy-start.4
  7.2 103.6 %all-gather.10.cloned.1.call-start = ((), (), s32[]{:S(2)}) async-start(), calls=%async_computation | async-start | bytes 8519680 | tf_op jit(solution)/shard_map/all_gather | solution.py:100
  7.3 7.3 %copy-start.1 = (bf16[256,2048]{1,0:T(8,128)(2,1)S(1)}, bf16[256,2048]{1,0:T(8,128)(2,1)}, u32[]{:S(2)}) copy-start(bf16[256,2048]{1,0:T(8,128)(2,1)} %param.18) | copy-start | bytes 3145732
  14.5 168.6 %all-gather.12.cloned.1.call-start = ((), (), s32[]{:S(2)}) async-start(), calls=%async_computation.1 | async-start | bytes 8519680 | tf_op jit(solution)/shard_map/all_gather | solution.py:101
  17.0 336.7 %all-gather.20.cloned.1.call-start = ((), (), s32[]{:S(2)}) async-start(), calls=%async_computation.6 | async-start | bytes 5242880 | tf_op jit(solution)/shard_map/all_gather | solution.py:126
  17.0 4.8 copy-start.5
  20.2 2.6 copy-start.3
  241.5 192.3 %all-gather.14.cloned.1.call-start = ((), (), s32[]{:S(2)}) async-start(), calls=%async_computation.2 | async-start | bytes 3194880 | tf_op jit(solution)/shard_map/all_gather | solution.py:134
  242.0 270.1 %all-gather.16.cloned.1.call-start = ((), (), s32[]{:S(2)}) async-start(), calls=%async_computation.3 | async-start | bytes 3194880 | tf_op jit(solution)/shard_map/all_gather | solution.py:139
  242.6 348.0 %all-gather.18.cloned.1.call-start = ((), (), s32[]{:S(2)}) async-start(), calls=%async_computation.4 | async-start | bytes 3194880 | tf_op jit(solution)/shard_map/all_gather | solution.py:144
  243.2 403.4 %all-reduce.2.cloned.1.call-start = ((), (), s32[]{:S(2)}) async-start(), calls=%async_computation.5 | async-start | bytes 2097152 | tf_op jit(solution)/shard_map/psum | solution.py:146
  353.7 80.1 %copy-start.6 = (f32[2048]{0:T(1024)S(1)}, f32[2048]{0:T(1024)}, u32[]{:S(2)}) copy-start(f32[2048]{0:T(1024)} %param.28) | copy-start | bytes 24580
Sparse Core Ops, SparseCore 0:
  14.6 84.7 all-gather.9
  102.7 80.3 all-gather.11
  241.6 112.0 all-gather.19
  356.3 77.4 all-gather.13
  436.4 75.7 all-gather.15
  514.8 75.7 all-gather.17
  597.0 49.5 all-reduce.1
